TPU v7x, 32 devices: a whole 2x2x4 slice. The times are simulated.
32 devices in a mesh: dp: 8 (over y, x, core), tensor: 4 (over z).
Axes of the slice: x: 2, y: 2, z: 4, core: 2. Of those that a mesh axis runs over, the one named last changes fastest.
Arguments:
- hidden: bfloat16 [1536, 16384], P('dp', 'tensor'), may hold values from -6 to 6
- cotangent: bfloat16 [1536, 16384], P('dp', 'tensor'), may hold values from -6 to 6
- blocks: bfloat16 [7, 64, 256, 256], P(None, 'tensor', 'dp'), may hold values from -0.125 to 0.125
- low_left: bfloat16 [16384, 128], P('tensor'), may hold values from -0.046875 to 0.046875
- low_right: bfloat16 [128, 16384], P(None, 'tensor'), may hold values from -0.5 to 0.5
Outputs:
- mixed_rows: bfloat16 [1536, 16384], P('dp', 'tensor')
- grad_hidden: bfloat16 [1536, 16384], P('dp', 'tensor')
- grad_blocks: float32 [7, 64, 256, 256], P(None, 'tensor', 'dp')
- grad_left: float32 [16384, 128], P('tensor')
- grad_right: float32 [128, 16384], P(None, 'tensor')
All inputs are finite; a program needn't handle non-finite values.
Results may differ from a plain program's by a relative error of at most 0.0095.
Values may be sent and summed in bfloat16 or wider, within the bound.
No kernel may reach another device: no remote copies, remote signals or barrier semaphores. Data moves between devices by JAX's collectives and lax.ppermute only.
A program may use at most 256 MiB of HBM per device.

v0:
```python
import jax
import jax.numpy as jnp
from jax import lax
from jax.sharding import PartitionSpec as P


def partner(value, axis, bit):
    return lax.ppermute(value, axis, [(i, i ^ 1 << bit) for i in range(lax.axis_size(axis))])


def flip_blocks(values, distance):
    array_shape = values.shape
    grouped = values.reshape(
        array_shape[:-2] + (array_shape[-2] // (2 * distance), 2, distance, array_shape[-1])
    )
    return grouped[..., ::-1, :, :].reshape(array_shape)


def per_device(hidden, cotangent, blocks, low_left, low_right):
    tok_rows, ff_local = hidden.shape
    blocks_here = blocks.shape[1]
    block_size = blocks.shape[3]
    local_bits = blocks_here.bit_length() - 1
    cross_bits = lax.axis_size("tensor").bit_length() - 1
    grad_scale = jnp.float32(1.0) / jnp.sqrt(jnp.float32(tok_rows * lax.axis_size("dp")))
    weights = lax.all_gather(blocks, "dp", axis=2, tiled=True)
    inputs_b = hidden.reshape(tok_rows, blocks_here, block_size)
    local_inputs = [inputs_b] + [
        flip_blocks(inputs_b, 2**level_idx) for level_idx in range(local_bits)
    ]
    remote_inputs = [partner(inputs_b, "tensor", bit_idx) for bit_idx in range(cross_bits)]
    stacked_in = jnp.stack(local_inputs + remote_inputs)
    mixed_blocks = jnp.einsum(
        "ktnb,knbc->tnc", stacked_in, weights, preferred_element_type=jnp.float32
    )
    partial_in = jnp.dot(hidden, low_left, preferred_element_type=jnp.float32)
    factor_b = lax.psum(partial_in, "tensor").astype(jnp.bfloat16)
    low_term = jnp.dot(factor_b, low_right, preferred_element_type=jnp.float32)
    mixed_rows = (mixed_blocks.reshape(tok_rows, ff_local) + low_term).astype(jnp.bfloat16)
    cot_b = cotangent.reshape(tok_rows, blocks_here, block_size)
    block_terms = (
        jnp.einsum("ktnb,tnc->knbc", stacked_in, cot_b, preferred_element_type=jnp.float32)
        * grad_scale
    )
    grad_blocks = lax.psum_scatter(
        block_terms.astype(jnp.bfloat16), "dp", scatter_dimension=2, tiled=True
    ).astype(jnp.float32)
    products = jnp.einsum("tnc,knbc->ktnb", cot_b, weights, preferred_element_type=jnp.float32)
    grad_in = products[0]
    for level_idx in range(local_bits):
        grad_in = grad_in + flip_blocks(products[1 + level_idx], 2**level_idx)
    for bit_idx in range(cross_bits):
        sent_terms = products[1 + local_bits + bit_idx]
        grad_in = grad_in + partner(sent_terms, "tensor", bit_idx)
    partial_back = jnp.einsum("tf,rf->tr", cotangent, low_right, preferred_element_type=jnp.float32)
    back_b = lax.psum(partial_back, "tensor").astype(jnp.bfloat16)
    low_back = jnp.einsum("tr,fr->tf", back_b, low_left, preferred_element_type=jnp.float32)
    grad_hidden = (grad_in.reshape(tok_rows, ff_local) + low_back).astype(jnp.bfloat16)
    part_left = (
        jnp.einsum("tf,tr->fr", hidden, back_b, preferred_element_type=jnp.float32) * grad_scale
    )
    part_right = (
        jnp.einsum("tr,tf->rf", factor_b, cotangent, preferred_element_type=jnp.float32)
        * grad_scale
    )
    grad_left, grad_right = lax.psum((part_left, part_right), "dp")
    return (mixed_rows, grad_hidden, grad_blocks, grad_left, grad_right)


def solution(mesh):
    placed = (
        P("dp", "tensor"),
        P("dp", "tensor"),
        P(None, "tensor", "dp", None),
        P("tensor", None),
        P(None, "tensor"),
    )
    return jax.shard_map(
        per_device,
        mesh=mesh,
        in_specs=placed,
        out_specs=(
            P("dp", "tensor"),
            P("dp", "tensor"),
            P(None, "tensor", "dp", None),
            P("tensor", None),
            P(None, "tensor"),
        ),
        check_vma=False,
    )
```

profile of v0, /device:TPU:0, one launch (start us, length us, event | category | flops | bytes accessed | tf_op | source)
XLA Modules:
  0.0 353.8 jit_solution(5965905838084927043)
XLA Ops:
  7.2 3.0 copy.29
  10.4 1.3 copy.59
  11.7 4.1 %collective-permute-start.1 = (bf16[192,16,256]{2,0,1:T(8,128)(2,1)}, bf16[192,16,256]{2,0,1:T(8,128)(2,1)}, u32[]{:S(2)}, u32[]{:S(2)}) collective-permute-start(bf16[192,16,256]{2,0,1:T(8,128)(2,1)} %bitcast.91), channel_id=1, source_target_pairs={{0,2},{1,3},{2,0},{3,1},{4,6},{5,7},{6,4},{7,5},{8,10},{9,11},{10,... | collective-permute-start | bytes 4718600 | tf_op jit(solution)/shard_map/ppermute | solution.py:8
  15.7 1.6 collective-permute-start
  17.3 0.6 fusion.18
  17.9 0.6 fusion.19
  18.4 82.4 %all-reduce.6 = (bf16[192,128]{1,0:T(8,128)(2,1)S(1)}, bf16[192,128]{1,0:T(8,128)(2,1)S(1)}) all-reduce(f32[192,128]{1,0:T(8,128)S(1)} %fusion.18, f32[192,128]{1,0:T(8,128)S(1)} %fusion.19), channel_id=1, replica_groups=mesh['dp'=8,'tensor'=4] {'tensor'}, use_global_device_ids=true, to_apply=%region_0.0 | all-reduce | flops 49152 | bytes 294912 | tf_op jit(solution)/shard_map/psum | solution.py:37
  100.9 3.2 convolution_multiply_fusion
  104.1 1.8 fusion.2
  106.1 2.4 reshape_reshape.14
  108.5 2.4 reshape_reshape.13
  110.9 2.4 reshape_reshape.12
  113.7 1.1 copy-done.4
  114.8 0.6 copy.25
  115.4 1.3 rev.27
  116.7 3.2 copy.24
  119.9 2.8 rev.26
  122.7 1.7 copy.23
  124.4 2.7 rev.25
  127.1 3.3 copy.22
  130.3 2.7 rev.24
  133.0 1.7 copy_dynamic-update-slice_fusion
  134.7 1.3 constant_dynamic-update-slice_fusion.3
  136.0 1.2 constant_dynamic-update-slice_fusion.2
  137.3 1.3 constant_dynamic-update-slice_fusion.1
  138.5 1.3 constant_dynamic-update-slice_fusion
  140.3 2.8 bitcast_dynamic-update-slice_fusion.1
  143.1 2.7 bitcast_dynamic-update-slice_fusion
  145.8 11.5 %fusion = bf16[7,16,256,256]{3,2,0,1:T(8,128)(2,1)} fusion(bf16[7,192,16,256]{3,1,0,2:T(8,128)(2,1)} %bitcast_dynamic-update-slice_fusion, bf16[192,16,256,1]{2,1,0,3:T(8,128)(2,1)S(1)} %bitcast.103), kind=kOutput, calls=%fused_computation.1 | convolution fusion | flops 2833252352 | bytes 27262976 | tf_op jit(solution)/shard_map/ktnb,tnc->knbc/dot_general | solution.py:42
  157.4 13.9 %convolution_bitcast_fusion = f32[7,192,16,256]{3,1,0,2:T(8,128)} fusion(bf16[7,16,256,256]{3,2,0,1:T(8,128)(2,1)} %all-gather.2.cloned.1.call-done, bf16[192,16,256,1]{2,1,0,3:T(8,128)(2,1)S(1)} %bitcast.104), kind=kOutput, calls=%fused_computation.2 | convolution fusion | flops 2818572288 | bytes 38273024 | tf_op jit(solution)/shard_map/tnc,knbc->ktnb/dot_general | solution.py:48
  171.2 13.8 %fusion.17 = (f32[1,192,16,256]{3,1,0,2:T(8,128)}, f32[192,16,256]{2,0,1:T(8,128)}, f32[1,192,16,256]{3,1,0,2:T(8,128)}, f32[1,192,16,256]{3,1,0,2:T(8,128)}, f3...) fusion(f32[7,192,16,256]{3,1,0,2:T(8,128)} %convolution_bitcast_fusion), kind=kLoop, calls=%fused_computation.35 | loop fusion | bytes 37748736 | tf_op jit(solution)/shard_map/slice | solution.py:51
  185.0 0.8 collective-permute-start.3
  185.8 2.2 fusion.20
  188.1 2.9 copy.37
  190.9 102.4 %reduce-scatter.2.cloned.1.call-done = bf16[7,16,32,256]{3,2,0,1:T(8,128)(2,1)} async-done(((bf16[7,16,256,256]{3,2,0,1:T(8,128)(2,1)}), bf16[7,16,32,256]{3,2,0,1:T(8,128)(2,1)}) %reduce-scatter.2.cloned.1.call-update) | async-done | bytes 1835024 | tf_op jit(solution)/shard_map/reduce_scatter | solution.py:45
  293.3 3.8 %copy.36 = f32[7,16,32,256]{3,2,1,0:T(8,128)} copy(bf16[7,16,32,256]{3,2,0,1:T(8,128)(2,1)} %reduce-scatter.2.cloned.1.call-done) | data formatting | bytes 5505024
  297.1 12.5 %convolution_bitcast_fusion.1 = f32[16,24,8,256]{3,2,1,0:T(8,128)S(1)} fusion(bf16[7,192,16,256]{3,1,0,2:T(8,128)(2,1)} %bitcast_dynamic-update-slice_fusion, bf16[7,16,256,256]{3,2,0,1:T(8,128)(2,1)} %all-gather.2.cloned.1.call-done), kind=kOutput, calls=%fused_computation.19 | convolution fusion | flops 2818572288 | bytes 28835840 | tf_op jit(solution)/shard_map/ktnb,knbc->tnc/dot_general | solution.py:33
  309.6 2.1 copy.48
  311.7 3.8 %rev.28 = f32[192,8,2,1,256]{4,0,2,1,3:T(8,128)} reverse(f32[192,8,2,1,256]{4,0,2,1,3:T(8,128)} %bitcast.100), dimensions={2} | reverse | bytes 6291456 | tf_op jit(solution)/shard_map/rev | solution.py:16
  315.5 3.9 %rev.31 = f32[192,1,2,8,256]{4,0,3,2,1:T(8,128)} reverse(f32[192,1,2,8,256]{4,0,3,2,1:T(8,128)} %bitcast.99), dimensions={2} | reverse | bytes 6291456 | tf_op jit(solution)/shard_map/rev | solution.py:16
  319.3 3.9 %rev.30 = f32[192,2,2,4,256]{4,0,3,2,1:T(8,128)} reverse(f32[192,2,2,4,256]{4,0,3,2,1:T(8,128)} %bitcast.98), dimensions={2} | reverse | bytes 6291456 | tf_op jit(solution)/shard_map/rev | solution.py:16
  323.2 4.0 %rev.29 = f32[192,4,2,2,256]{4,0,3,2,1:T(8,128)} reverse(f32[192,4,2,2,256]{4,0,3,2,1:T(8,128)} %bitcast.97), dimensions={2} | reverse | bytes 6291456 | tf_op jit(solution)/shard_map/rev | solution.py:16
  327.2 3.7 %fusion.1 = bf16[192,4096]{1,0:T(8,128)(2,1)} fusion(f32[192,4096]{1,0:T(8,128)} %bitcast.101, bf16[128,4096]{1,0:T(8,128)(2,1)S(1)} %copy-done.14, bf16[192,128]{1,0:T(8,128)(2,1)S(1)} %get-tuple-element.17), kind=kOutput, calls=%fused_computation.4 | convolution fusion | flops 202899456 | bytes 5816320 | tf_op jit(solution)/shard_map/dot_general | solution.py:38
  331.0 10.0 %fusion.9 = f32[16,24,8,256]{3,2,1,0:T(8,128)} fusion(f32[192,16,256]{2,0,1:T(8,128)} %collective-permute-done.3, f32[192,16,256]{2,0,1:T(8,128)} %collective-permute-done.2, f32[7,192,16,256]{3,1,0,2:T(8,128)} %convolution_bitcast_fusion, f32[192,1,2,8,256]{4,0,3,2,1:T(8,128)} %rev.31, f32[192,2,2,4,256]{4,0,3,2,1:T(8,128)} %rev.30, ...), kind=kLoop, calls=%fused_computation.17 | loop fusion | flops 4718592 | bytes 25165824
  340.9 2.4 copy.49
  343.8 1.5 add_convert_fusion
  345.3 0.6 copy-done.15
  345.9 1.3 copy.72
  (45 shorter events, 1.7 us)
Async XLA Ops:
  7.2 10.1 %copy-start = (bf16[4096,128]{1,0:T(8,128)(2,1)S(1)}, bf16[4096,128]{1,0:T(8,128)(2,1)}, u32[]{:S(2)}) copy-start(bf16[4096,128]{1,0:T(8,128)(2,1)} %param.8) | copy-start | bytes 3145732
  7.2 3.2 copy-start.1
  7.2 150.2 %all-gather.2.cloned.1.call-start = ((), (), s32[]{:S(2)}) async-start(), calls=%async_computation.1 | async-start | bytes 16515072 | tf_op jit(solution)/shard_map/all_gather | solution.py:26
  10.3 177.8 %all-reduce.5.cloned.1.call-start = ((), (), s32[]{:S(2)}) async-start(), calls=%async_computation.3 | async-start | bytes 8388608 | tf_op jit(solution)/shard_map/psum | solution.py:66
  10.3 7.5 %copy-start.2 = (bf16[192,4096]{1,0:T(8,128)(2,1)S(1)}, bf16[192,4096]{1,0:T(8,128)(2,1)}, u32[]{:S(2)}) copy-start(bf16[192,4096]{1,0:T(8,128)(2,1)} %param.6) | copy-start | bytes 4718596
  10.4 7.5 %copy-start.13 = (bf16[128,4096]{1,0:T(8,128)(2,1)S(1)}, bf16[128,4096]{1,0:T(8,128)(2,1)}, u32[]{:S(2)}) copy-start(bf16[128,4096]{1,0:T(8,128)(2,1)} %param.9) | copy-start | bytes 3145732
  11.7 131.4 %collective-permute-start.1 = (bf16[192,16,256]{2,0,1:T(8,128)(2,1)}, bf16[192,16,256]{2,0,1:T(8,128)(2,1)}, u32[]{:S(2)}, u32[]{:S(2)}) collective-permute-start(bf16[192,16,256]{2,0,1:T(8,128)(2,1)} %bitcast.91), channel_id=1, source_target_pairs={{0,2},{1,3},{2,0},{3,1},{4,6},{5,7},{6,4},{7,5},{8,10},{9,11},{10,... | collective-permute-start | bytes 4718600 | tf_op jit(solution)/shard_map/ppermute | solution.py:8
  15.7 124.6 %collective-permute-start = (bf16[192,16,256]{2,0,1:T(8,128)(2,1)}, bf16[192,16,256]{2,0,1:T(8,128)(2,1)}, u32[]{:S(2)}, u32[]{:S(2)}) collective-permute-start(bf16[192,16,256]{2,0,1:T(8,128)(2,1)} %bitcast.91), channel_id=1, source_target_pairs={{0,1},{1,0},{2,3},{3,2},{4,5},{5,4},{6,7},{7,6},{8,9},{9,8},{10,11... | collective-permute-start | bytes 4718600 | tf_op jit(solution)/shard_map/ppermute | solution.py:8
  105.9 187.4 %reduce-scatter.2.cloned.1.call-start = ((), (), s32[]{:S(2)}) async-start(), calls=%async_computation.2 | async-start | bytes 16515072 | tf_op jit(solution)/shard_map/reduce_scatter | solution.py:45
  113.7 1.1 copy-start.4
  116.7 6.0 %copy-start.11 = (bf16[192,4,2,2,256]{4,3,2,1,0:T(2,128)(2,1)S(1)}, bf16[192,4,2,2,256]{4,3,2,1,0:T(2,128)(2,1)}, u32[]{:S(2)}) copy-start(bf16[192,4,2,2,256]{4,3,2,1,0:T(2,128)(2,1)} %reshape_reshape.13) | copy-start | bytes 4718596
  127.1 6.0 %copy-start.5 = (bf16[24,8,16,256]{3,2,1,0:T(8,128)(2,1)S(1)}, bf16[24,8,16,256]{3,2,1,0:T(8,128)(2,1)}, u32[]{:S(2)}) copy-start(bf16[24,8,16,256]{3,2,1,0:T(8,128)(2,1)} %copy-done.4) | copy-start | bytes 4718596
  133.0 1.7 copy-start.12
  133.0 3.0 copy-start.10
  134.7 2.5 copy-start.9
  136.0 2.5 copy-start.8
  137.3 2.6 copy-start.3
  185.0 146.0 %collective-permute-start.3 = (f32[192,16,256]{2,0,1:T(8,128)}, f32[192,16,256]{2,0,1:T(8,128)}, u32[]{:S(2)}, u32[]{:S(2)}) collective-permute-start(f32[192,16,256]{2,0,1:T(8,128)} %get-tuple-element.20), channel_id=1, source_target_pairs={{0,2},{1,3},{2,0},{3,1},{4,6},{5,7},{6,4},{7,5},{8,10},{9,11},{10,... | collective-permute-start | bytes 9437192 | tf_op jit(solution)/shard_map/ppermute | solution.py:8
  185.8 145.1 %collective-permute-start.2 = (f32[192,16,256]{2,0,1:T(8,128)}, f32[192,16,256]{2,0,1:T(8,128)}, u32[]{:S(2)}, u32[]{:S(2)}) collective-permute-start(f32[192,16,256]{2,0,1:T(8,128)} %get-tuple-element.24), channel_id=1, source_target_pairs={{0,1},{1,0},{2,3},{3,2},{4,5},{5,4},{6,7},{7,6},{8,9},{9,8},{10,11... | collective-permute-start | bytes 9437192 | tf_op jit(solution)/shard_map/ppermute | solution.py:8
  323.2 4.0 %copy-start.14 = (bf16[128,4096]{1,0:T(8,128)(2,1)S(1)}, bf16[128,4096]{1,0:T(8,128)(2,1)}, u32[]{:S(2)}) copy-start(bf16[128,4096]{1,0:T(8,128)(2,1)} %param.9) | copy-start | bytes 3145732
  327.2 3.8 %copy-start.6 = (f32[192,8,2,1,256]{4,0,2,1,3:T(8,128)S(1)}, f32[192,8,2,1,256]{4,0,2,1,3:T(8,128)}, u32[]{:S(2)}) copy-start(f32[192,8,2,1,256]{4,0,2,1,3:T(8,128)} %rev.28) | copy-start | bytes 9437188
  340.9 2.8 copy-start.7
  343.8 2.2 copy-start.15
Sparse Core Ops, SparseCore 0:
  10.5 83.6 all-gather.1
  106.0 79.6 all-reduce.4
  189.7 103.6 reduce-scatter.1
where the time goes:
time: 354 us
  waiting for transfers between devices  102 us (29%)
  local copies, waits for them, and re-layouts  86.7 us (24%)
  blocking collectives  82.4 us (23%)
  matrix products  50 us (14%)
  between operations  13.9 us (4%)
  other arithmetic  11.5 us (3%)
  starting transfers between devices  6.77 us (2%)
    reduce_scatter x1, waiting for transfers between devices, per_device(): lax.psum_scatter(block_terms.astype(jnp.bfloat16), 'dp', scatter_dimensio...  102 us
    psum x1, blocking collectives, per_device(): factor_b = lax.psum(partial_in, 'tensor').astype(jnp.bfloat16)  82.4 us
    rev x8, local copies, waits for them, and re-layouts, flip_blocks(): return grouped[..., ::-1, :, :].reshape(array_shape)  24.9 us
    unnamed x44, local copies, waits for them, and re-layouts  23.7 us
    another operation x7, local copies, waits for them, and re-layouts, flip_blocks(): values.reshape(array_shape[:-2] + (array_shape[-2] // (2 * distance), 2,...  15.8 us
    dot_general x1, matrix products, per_device(): jnp.einsum('tnc,knbc->ktnb', cot_b, weights, preferred_element_type=jnp.f...  13.9 us
    slice x1, local copies, waits for them, and re-layouts, per_device(): grad_in = grad_in + flip_blocks(products[1 + level_idx], 2 ** level_idx)  13.8 us
    dot_general x1, matrix products, per_device(): jnp.einsum('ktnb,knbc->tnc', stacked_in, weights, preferred_element_type=...  12.5 us
  transfers between devices with their start and end apart: 7, of which 1 were waited for; matrix products, arithmetic and copies ran while one was open for 36% of the time, Pallas kernels for 0%

commit v1 on v0

--- a/solution.py
+++ b/solution.py
@@ -2,6 +2,10 @@
 import jax.numpy as jnp
 from jax import lax
 from jax.sharding import PartitionSpec as P
+
+
+def extend_block_all(local_x):
+    return jnp.sum(lax.all_gather(local_x, "tensor"), axis=0)
 
 
 def partner(value, axis, bit):
@@ -34,7 +38,7 @@
         "ktnb,knbc->tnc", stacked_in, weights, preferred_element_type=jnp.float32
     )
     partial_in = jnp.dot(hidden, low_left, preferred_element_type=jnp.float32)
-    factor_b = lax.psum(partial_in, "tensor").astype(jnp.bfloat16)
+    factor_b = extend_block_all(partial_in).astype(jnp.bfloat16)
     low_term = jnp.dot(factor_b, low_right, preferred_element_type=jnp.float32)
     mixed_rows = (mixed_blocks.reshape(tok_rows, ff_local) + low_term).astype(jnp.bfloat16)
     cot_b = cotangent.reshape(tok_rows, blocks_here, block_size)

time: 354 us -> 369 us (1.042)
  blocking collectives: 82.4 us -> 97.1 us
    all_gather x0 -> x1, blocking collectives: none -> 77 us  [extend_block_all(): return jnp.sum(lax.all_gather(local_x, 'tensor'), axis=0)]
    psum x1, blocking collectives: 82.4 us -> 20.2 us  [per_device(): back_b = lax.psum(partial_back, 'tensor').astype(jnp.bfloat16)]
  transfers between devices with their start and end apart: 7 -> 7, of which waited for: 1 -> 1; matrix products, arithmetic and copies ran while one was open for 36% -> 35% of each run, Pallas kernels for 0% -> 0%
where the time goes in v1:
time: 369 us; the launch traced here: 368 us
  waiting for transfers between devices  102 us (28%)
  blocking collectives  97.1 us (26%)
  local copies, waits for them, and re-layouts  86.8 us (24%)
  matrix products  50.2 us (14%)
  between operations  13.9 us (4%)
  other arithmetic  11.5 us (3%)
  starting transfers between devices  6.58 us (2%)
    reduce_scatter x1, waiting for transfers between devices, per_device(): lax.psum_scatter(block_terms.astype(jnp.bfloat16), 'dp', scatter_dimensio...  102 us
    all_gather x1, blocking collectives, extend_block_all(): return jnp.sum(lax.all_gather(local_x, 'tensor'), axis=0)  77 us
    rev x8, local copies, waits for them, and re-layouts, flip_blocks(): return grouped[..., ::-1, :, :].reshape(array_shape)  24.9 us
    unnamed x44, local copies, waits for them, and re-layouts  23.7 us
    psum x1, blocking collectives, per_device(): back_b = lax.psum(partial_back, 'tensor').astype(jnp.bfloat16)  20.2 us
    another operation x7, local copies, waits for them, and re-layouts, flip_blocks(): values.reshape(array_shape[:-2] + (array_shape[-2] // (2 * distance), 2,...  15.9 us
    dot_general x1, matrix products, per_device(): jnp.einsum('tnc,knbc->ktnb', cot_b, weights, preferred_element_type=jnp.f...  13.9 us
    slice x1, local copies, waits for them, and re-layouts, per_device(): grad_in = grad_in + flip_blocks(products[1 + level_idx], 2 ** level_idx)  13.8 us
  transfers between devices with their start and end apart: 7, of which 1 were waited for; matrix products, arithmetic and copies ran while one was open for 35% of the time, Pallas kernels for 0%

profile of v1, /device:TPU:0, one launch (start us, length us, event | category | flops | bytes accessed | tf_op | source)
XLA Modules:
  0.0 368.4 jit_solution(2973268063444798598)
XLA Ops:
  7.2 3.0 copy.29
  10.4 1.3 copy.59
  11.7 4.0 %collective-permute-start.1 = (bf16[192,16,256]{2,0,1:T(8,128)(2,1)}, bf16[192,16,256]{2,0,1:T(8,128)(2,1)}, u32[]{:S(2)}, u32[]{:S(2)}) collective-permute-start(bf16[192,16,256]{2,0,1:T(8,128)(2,1)} %bitcast.92), channel_id=1, source_target_pairs={{0,2},{1,3},{2,0},{3,1},{4,6},{5,7},{6,4},{7,5},{8,10},{9,11},{10,... | collective-permute-start | bytes 4718600 | tf_op jit(solution)/shard_map/ppermute | solution.py:12
  15.7 1.6 collective-permute-start
  17.3 0.6 fusion.18
  17.8 77.0 %all-gather = f32[768,128]{1,0:T(8,128)S(1)} all-gather(f32[192,128]{1,0:T(8,128)S(1)} %fusion.18), channel_id=2, replica_groups=mesh['dp'=8,'tensor'=4] {'tensor'}, dimensions={0}, use_global_device_ids=true | all-gather | bytes 491520 | tf_op jit(solution)/shard_map/all_gather | solution.py:8
  94.9 3.3 convolution_multiply_fusion
  98.2 0.6 fusion.19
  98.8 20.2 %psum.21 = bf16[192,128]{1,0:T(8,128)(2,1)S(1)} all-reduce(f32[192,128]{1,0:T(8,128)S(1)} %fusion.19), channel_id=1, replica_groups=mesh['dp'=8,'tensor'=4] {'tensor'}, use_global_device_ids=true, to_apply=%region_1.0 | all-reduce | flops 24576 | bytes 147456 | tf_op jit(solution)/shard_map/psum | solution.py:60
  119.0 1.8 fusion.2
  121.0 2.4 reshape_reshape.14
  123.4 2.4 reshape_reshape.13
  125.8 2.4 reshape_reshape.12
  128.6 1.1 copy-done.4
  130.3 1.3 rev.27
  131.6 3.3 copy.24
  134.9 2.7 rev.26
  137.6 1.7 copy.23
  139.3 2.7 rev.25
  142.0 3.2 copy.22
  145.2 2.7 rev.24
  147.9 1.7 copy_dynamic-update-slice_fusion
  149.6 1.3 constant_dynamic-update-slice_fusion.3
  150.9 1.3 constant_dynamic-update-slice_fusion.2
  152.2 1.3 constant_dynamic-update-slice_fusion.1
  153.5 1.3 constant_dynamic-update-slice_fusion
  155.2 2.7 bitcast_dynamic-update-slice_fusion.1
  158.0 2.7 bitcast_dynamic-update-slice_fusion
  160.7 11.5 %fusion = bf16[7,16,256,256]{3,2,0,1:T(8,128)(2,1)} fusion(bf16[7,192,16,256]{3,1,0,2:T(8,128)(2,1)} %bitcast_dynamic-update-slice_fusion, bf16[192,16,256,1]{2,1,0,3:T(8,128)(2,1)S(1)} %bitcast.104), kind=kOutput, calls=%fused_computation.1 | convolution fusion | flops 2833252352 | bytes 27262976 | tf_op jit(solution)/shard_map/ktnb,tnc->knbc/dot_general | solution.py:46
  172.2 13.9 %convolution_bitcast_fusion = f32[7,192,16,256]{3,1,0,2:T(8,128)} fusion(bf16[7,16,256,256]{3,2,0,1:T(8,128)(2,1)} %all-gather.3.cloned.1.call-done, bf16[192,16,256,1]{2,1,0,3:T(8,128)(2,1)S(1)} %bitcast.105), kind=kOutput, calls=%fused_computation.2 | convolution fusion | flops 2818572288 | bytes 38273024 | tf_op jit(solution)/shard_map/tnc,knbc->ktnb/dot_general | solution.py:52
  186.1 13.8 %fusion.17 = (f32[1,192,16,256]{3,1,0,2:T(8,128)}, f32[192,16,256]{2,0,1:T(8,128)}, f32[1,192,16,256]{3,1,0,2:T(8,128)}, f32[1,192,16,256]{3,1,0,2:T(8,128)}, f3...) fusion(f32[7,192,16,256]{3,1,0,2:T(8,128)} %convolution_bitcast_fusion), kind=kLoop, calls=%fused_computation.35 | loop fusion | bytes 37748736 | tf_op jit(solution)/shard_map/slice | solution.py:55
  199.9 0.7 collective-permute-start.3
  200.6 2.2 fusion.20
  202.8 2.9 copy.37
  205.7 102.2 %reduce-scatter.2.cloned.1.call-done = bf16[7,16,32,256]{3,2,0,1:T(8,128)(2,1)} async-done(((bf16[7,16,256,256]{3,2,0,1:T(8,128)(2,1)}), bf16[7,16,32,256]{3,2,0,1:T(8,128)(2,1)}) %reduce-scatter.2.cloned.1.call-update) | async-done | bytes 1835024 | tf_op jit(solution)/shard_map/reduce_scatter | solution.py:49
  307.9 3.8 %copy.36 = f32[7,16,32,256]{3,2,1,0:T(8,128)} copy(bf16[7,16,32,256]{3,2,0,1:T(8,128)(2,1)} %reduce-scatter.2.cloned.1.call-done) | data formatting | bytes 5505024
  311.6 12.5 %convolution_bitcast_fusion.1 = f32[16,24,8,256]{3,2,1,0:T(8,128)S(1)} fusion(bf16[7,192,16,256]{3,1,0,2:T(8,128)(2,1)} %bitcast_dynamic-update-slice_fusion, bf16[7,16,256,256]{3,2,0,1:T(8,128)(2,1)} %all-gather.3.cloned.1.call-done), kind=kOutput, calls=%fused_computation.19 | convolution fusion | flops 2818572288 | bytes 28835840 | tf_op jit(solution)/shard_map/ktnb,knbc->tnc/dot_general | solution.py:37
  324.2 2.1 copy.48
  326.3 3.8 %rev.28 = f32[192,8,2,1,256]{4,0,2,1,3:T(8,128)} reverse(f32[192,8,2,1,256]{4,0,2,1,3:T(8,128)} %bitcast.101), dimensions={2} | reverse | bytes 6291456 | tf_op jit(solution)/shard_map/rev | solution.py:20
  330.1 3.8 %rev.31 = f32[192,1,2,8,256]{4,0,3,2,1:T(8,128)} reverse(f32[192,1,2,8,256]{4,0,3,2,1:T(8,128)} %bitcast.100), dimensions={2} | reverse | bytes 6291456 | tf_op jit(solution)/shard_map/rev | solution.py:20
  333.9 3.9 %rev.30 = f32[192,2,2,4,256]{4,0,3,2,1:T(8,128)} reverse(f32[192,2,2,4,256]{4,0,3,2,1:T(8,128)} %bitcast.99), dimensions={2} | reverse | bytes 6291456 | tf_op jit(solution)/shard_map/rev | solution.py:20
  337.8 4.0 %rev.29 = f32[192,4,2,2,256]{4,0,3,2,1:T(8,128)} reverse(f32[192,4,2,2,256]{4,0,3,2,1:T(8,128)} %bitcast.98), dimensions={2} | reverse | bytes 6291456 | tf_op jit(solution)/shard_map/rev | solution.py:20
  341.8 3.7 %fusion.1 = bf16[192,4096]{1,0:T(8,128)(2,1)} fusion(f32[192,4096]{1,0:T(8,128)} %bitcast.102, bf16[128,4096]{1,0:T(8,128)(2,1)S(1)} %copy-done.14, bf16[192,128]{1,0:T(8,128)(2,1)S(1)} %reduce_sum.9), kind=kOutput, calls=%fused_computation.4 | convolution fusion | flops 202899456 | bytes 5816320 | tf_op jit(solution)/shard_map/dot_general | solution.py:42
  345.5 10.0 %fusion.9 = f32[16,24,8,256]{3,2,1,0:T(8,128)} fusion(f32[192,16,256]{2,0,1:T(8,128)} %collective-permute-done.3, f32[192,16,256]{2,0,1:T(8,128)} %collective-permute-done.2, f32[7,192,16,256]{3,1,0,2:T(8,128)} %convolution_bitcast_fusion, f32[192,1,2,8,256]{4,0,3,2,1:T(8,128)} %rev.31, f32[192,2,2,4,256]{4,0,3,2,1:T(8,128)} %rev.30, ...), kind=kLoop, calls=%fused_computation.17 | loop fusion | flops 4718592 | bytes 25165824
  355.5 2.4 copy.49
  358.4 1.5 add_convert_fusion
  359.9 0.6 copy-done.15
  360.5 1.3 copy.68
  (47 shorter events, 2.3 us)
Async XLA Ops:
  7.2 10.1 %copy-start = (bf16[4096,128]{1,0:T(8,128)(2,1)S(1)}, bf16[4096,128]{1,0:T(8,128)(2,1)}, u32[]{:S(2)}) copy-start(bf16[4096,128]{1,0:T(8,128)(2,1)} %param.8) | copy-start | bytes 3145732
  7.2 3.2 copy-start.1
  7.2 165.0 %all-gather.3.cloned.1.call-start = ((), (), s32[]{:S(2)}) async-start(), calls=%async_computation.1 | async-start | bytes 16515072 | tf_op jit(solution)/shard_map/all_gather | solution.py:30
  10.3 192.5 %all-reduce.3.cloned.1.call-start = ((), (), s32[]{:S(2)}) async-start(), calls=%async_computation.3 | async-start | bytes 8388608 | tf_op jit(solution)/shard_map/psum | solution.py:70
  11.7 146.3 %collective-permute-start.1 = (bf16[192,16,256]{2,0,1:T(8,128)(2,1)}, bf16[192,16,256]{2,0,1:T(8,128)(2,1)}, u32[]{:S(2)}, u32[]{:S(2)}) collective-permute-start(bf16[192,16,256]{2,0,1:T(8,128)(2,1)} %bitcast.92), channel_id=1, source_target_pairs={{0,2},{1,3},{2,0},{3,1},{4,6},{5,7},{6,4},{7,5},{8,10},{9,11},{10,... | collective-permute-start | bytes 4718600 | tf_op jit(solution)/shard_map/ppermute | solution.py:12
  15.7 139.6 %collective-permute-start = (bf16[192,16,256]{2,0,1:T(8,128)(2,1)}, bf16[192,16,256]{2,0,1:T(8,128)(2,1)}, u32[]{:S(2)}, u32[]{:S(2)}) collective-permute-start(bf16[192,16,256]{2,0,1:T(8,128)(2,1)} %bitcast.92), channel_id=1, source_target_pairs={{0,1},{1,0},{2,3},{3,2},{4,5},{5,4},{6,7},{7,6},{8,9},{9,8},{10,11... | collective-permute-start | bytes 4718600 | tf_op jit(solution)/shard_map/ppermute | solution.py:12
  94.9 3.4 copy-start.2
  94.9 3.4 copy-start.13
  120.8 187.1 %reduce-scatter.2.cloned.1.call-start = ((), (), s32[]{:S(2)}) async-start(), calls=%async_computation.2 | async-start | bytes 16515072 | tf_op jit(solution)/shard_map/reduce_scatter | solution.py:49
  128.6 1.1 copy-start.4
  131.6 6.0 %copy-start.11 = (bf16[192,4,2,2,256]{4,3,2,1,0:T(2,128)(2,1)S(1)}, bf16[192,4,2,2,256]{4,3,2,1,0:T(2,128)(2,1)}, u32[]{:S(2)}) copy-start(bf16[192,4,2,2,256]{4,3,2,1,0:T(2,128)(2,1)} %reshape_reshape.13) | copy-start | bytes 4718596
  142.0 5.9 %copy-start.5 = (bf16[24,8,16,256]{3,2,1,0:T(8,128)(2,1)S(1)}, bf16[24,8,16,256]{3,2,1,0:T(8,128)(2,1)}, u32[]{:S(2)}) copy-start(bf16[24,8,16,256]{3,2,1,0:T(8,128)(2,1)} %copy-done.4) | copy-start | bytes 4718596
  147.9 1.7 copy-start.12
  147.9 3.0 copy-start.10
  149.6 2.6 copy-start.9
  150.9 2.7 copy-start.8
  152.2 2.6 copy-start.3
  199.9 145.6 %collective-permute-start.3 = (f32[192,16,256]{2,0,1:T(8,128)}, f32[192,16,256]{2,0,1:T(8,128)}, u32[]{:S(2)}, u32[]{:S(2)}) collective-permute-start(f32[192,16,256]{2,0,1:T(8,128)} %get-tuple-element.18), channel_id=1, source_target_pairs={{0,2},{1,3},{2,0},{3,1},{4,6},{5,7},{6,4},{7,5},{8,10},{9,11},{10,... | collective-permute-start | bytes 9437192 | tf_op jit(solution)/shard_map/ppermute | solution.py:12
  200.6 145.0 %collective-permute-start.2 = (f32[192,16,256]{2,0,1:T(8,128)}, f32[192,16,256]{2,0,1:T(8,128)}, u32[]{:S(2)}, u32[]{:S(2)}) collective-permute-start(f32[192,16,256]{2,0,1:T(8,128)} %get-tuple-element.22), channel_id=1, source_target_pairs={{0,1},{1,0},{2,3},{3,2},{4,5},{5,4},{6,7},{7,6},{8,9},{9,8},{10,11... | collective-permute-start | bytes 9437192 | tf_op jit(solution)/shard_map/ppermute | solution.py:12
  337.8 4.0 %copy-start.14 = (bf16[128,4096]{1,0:T(8,128)(2,1)S(1)}, bf16[128,4096]{1,0:T(8,128)(2,1)}, u32[]{:S(2)}) copy-start(bf16[128,4096]{1,0:T(8,128)(2,1)} %param.9) | copy-start | bytes 3145732
  341.8 3.8 %copy-start.6 = (f32[192,8,2,1,256]{4,0,2,1,3:T(8,128)S(1)}, f32[192,8,2,1,256]{4,0,2,1,3:T(8,128)}, u32[]{:S(2)}) copy-start(f32[192,8,2,1,256]{4,0,2,1,3:T(8,128)} %rev.28) | copy-start | bytes 9437188
  355.5 2.8 copy-start.7
  358.4 2.2 copy-start.15
Sparse Core Ops, SparseCore 0:
  10.5 83.6 all-gather.2
  120.9 79.3 all-reduce.2
  204.2 103.6 reduce-scatter.1
